TPU v7x, 32 devices: a whole 2x2x4 slice. The times are simulated.
32 devices in a mesh: radial: 8 (over y, x, core), mode: 4 (over z).
Axes of the slice: x: 2, y: 2, z: 4, core: 2. Of those that a mesh axis runs over, the one named last changes fastest.
Arguments:
- scalar_field: float32 [256, 64, 2, 384], P('radial', 'mode'), may hold values from -48 to 48
- radial_flow: float32 [256, 64, 2, 384], P('radial', 'mode'), may hold values from -6 to 6
- legendre: bfloat16 [64, 384, 768], P('mode'), may hold values from -0.3125 to 0.3125
- diffusivity: float32 [256], P('radial'), may hold values from 1000 to 100000
Outputs:
- field_new: float32 [256, 64, 2, 384], P('radial', 'mode')
All inputs are finite; a program needn't handle non-finite values.
Results may differ from a plain program's by a relative error of at most 0.0071.
Values may be sent and summed in bfloat16 or wider, within the bound.
A program may use at most 128 MiB of HBM per device.

v0:
```python
import math

import jax
import jax.numpy as jnp
from jax import lax
from jax.sharding import PartitionSpec as P

NLON = 1536


def prefix_2(value, axis, join, neutral, backward):
    count, mine = (lax.axis_size(axis), lax.axis_index(axis))
    pieces = jax.tree.map(lambda part: lax.all_gather(part, axis), value)
    if backward:
        pieces = jax.tree.map(lambda part: part[::-1], pieces)
        mine = count - 1 - mine
    total = jax.tree.map(
        lambda part, zero: jnp.full_like(part, 0) + jnp.asarray(zero, part.dtype), value, neutral
    )

    def hop(position, total):
        longer = join(total, jax.tree.map(lambda part: part[position], pieces))
        return jax.tree.map(lambda new, old: jnp.where(position < mine, new, old), longer, total)

    return lax.fori_loop(0, count - 1, hop, total)


def longitude_tables(orders, points):
    order_ids = jnp.arange(orders, dtype=jnp.int32)
    point_ids = jnp.arange(points, dtype=jnp.int32)
    phase = order_ids[:, None] * point_ids[None, :] % points
    angle = phase.astype(jnp.float32) * (2.0 * math.pi / points)
    cosine = jnp.cos(angle)
    sine_part = jnp.sin(angle)
    paired = jnp.stack([cosine, -sine_part], axis=1)
    synth_table = (paired / math.sqrt(orders)).astype(jnp.bfloat16)
    analysis_table = (paired * math.sqrt(2.0 / points)).astype(jnp.bfloat16)
    return (synth_table, analysis_table)


def normalized(matrix):
    largest = jnp.max(jnp.abs(matrix), axis=(0, 1))
    return matrix / largest


def combine_maps(earlier, later):
    return normalized(jnp.sum(later[:, :, None] * earlier[None, :, :], axis=1))


def combine_affine(earlier, later):
    return (later[0] + later[1][:, None, :] * earlier[0], later[1] * earlier[1])


def on_device(scalar_field, radial_flow, legendre, diffusivity):
    shells, ord_dev, halves, degrees = scalar_field.shape
    orders = ord_dev * lax.axis_size("mode")
    synth_table, analysis_table = longitude_tables(orders, NLON)
    field_lat = jnp.einsum(
        "rmcj,mjt->rmct",
        scalar_field.astype(jnp.bfloat16),
        legendre,
        preferred_element_type=jnp.float32,
    ).astype(jnp.bfloat16)
    flow_lat = jnp.einsum(
        "rmcj,mjt->rmct",
        radial_flow.astype(jnp.bfloat16),
        legendre,
        preferred_element_type=jnp.float32,
    ).astype(jnp.bfloat16)
    field_piece = lax.all_to_all(field_lat, "mode", split_axis=3, concat_axis=1, tiled=True)
    flow_piece = lax.all_to_all(flow_lat, "mode", split_axis=3, concat_axis=1, tiled=True)
    field_grid = jnp.einsum(
        "rmct,mcp->rtp", field_piece, synth_table, preferred_element_type=jnp.float32
    )
    flow_grid = jnp.einsum(
        "rmct,mcp->rtp", flow_piece, synth_table, preferred_element_type=jnp.float32
    )
    product = (field_grid * flow_grid).astype(jnp.bfloat16)
    modes_grid = jnp.einsum(
        "rtp,mcp->rmct", product, analysis_table, preferred_element_type=jnp.float32
    ).astype(jnp.bfloat16)
    spectral_back = lax.all_to_all(modes_grid, "mode", split_axis=1, concat_axis=3, tiled=True)
    forcing = jnp.einsum(
        "rmct,mjt->rmcj", spectral_back, legendre, preferred_element_type=jnp.float32
    )
    right_side = scalar_field + forcing
    radial_index = lax.axis_index("radial")
    nr_total = shells * lax.axis_size("radial")
    offset = nr_total * 7 // 13
    order_ids = (jnp.arange(ord_dev, dtype=jnp.int32) + lax.axis_index("mode") * ord_dev).astype(
        jnp.float32
    )
    degree = order_ids[:, None] + jnp.arange(degrees, dtype=jnp.float32)[None, :]
    angular = degree * (degree + 1.0)
    global_shells = radial_index * shells + jnp.arange(shells, dtype=jnp.int32)

    def coefficients(kappa_shell, shell_index):
        lower = jnp.where(shell_index > 0, -kappa_shell, 0.0)
        upper = jnp.where(shell_index < nr_total - 1, -kappa_shell, 0.0)
        radius = (offset + shell_index).astype(jnp.float32)
        diagonal = 1.0 + 2.0 * kappa_shell + kappa_shell * angular / (radius * radius)
        return (lower, upper, diagonal)

    identity = jnp.broadcast_to(
        jnp.eye(4, dtype=jnp.float32)[:, :, None, None], (4, 4, ord_dev, degrees)
    )

    def compose(composite, inputs):
        kappa_shell, source, shell_index = inputs
        lower, upper, diagonal = coefficients(kappa_shell, shell_index)
        new_rows = jnp.stack(
            [
                upper * composite[3],
                -lower * composite[1] + source[:, 0, :] * composite[3],
                -lower * composite[2] + source[:, 1, :] * composite[3],
                -lower * composite[0] + diagonal * composite[3],
            ]
        )
        return (normalized(new_rows), None)

    transfer, _ = lax.scan(compose, identity, (diffusivity, right_side, global_shells))
    prefix = prefix_2(transfer, "radial", combine_maps, identity, False)
    incoming = prefix[:, 3]
    ratio_start = incoming[0] / incoming[3]
    value_start = jnp.stack([incoming[1], incoming[2]], axis=1) / incoming[3][:, None, :]

    def sweep(carry, inputs):
        ratio_prev, value_prev = carry
        kappa_shell, source, shell_index = inputs
        lower, upper, diagonal = coefficients(kappa_shell, shell_index)
        pivot = diagonal - lower * ratio_prev
        ratio_now = upper / pivot
        value_now = (source - lower * value_prev) / pivot[:, None, :]
        return ((ratio_now, value_now), (ratio_now, value_now))

    _, (ratios, values) = lax.scan(
        sweep, (ratio_start, value_start), (diffusivity, right_side, global_shells)
    )

    def back_compose(carry, inputs):
        alpha, slope = carry
        ratio_now, value_now = inputs
        alpha = value_now - ratio_now[:, None, :] * alpha
        slope = -ratio_now * slope
        return ((alpha, slope), (alpha, slope))

    blank_value = jnp.zeros((ord_dev, halves, degrees), jnp.float32)
    unity = jnp.ones((ord_dev, degrees), jnp.float32)
    (alpha_dev, slope_dev), (alpha_all, slope_all) = lax.scan(
        back_compose, (blank_value, unity), (ratios, values), reverse=True
    )
    beyond, _ = prefix_2(
        (alpha_dev, slope_dev), "radial", combine_affine, (blank_value, unity), True
    )
    return alpha_all + slope_all[:, :, None, :] * beyond[None]


def solution(mesh):
    return jax.shard_map(
        on_device,
        mesh=mesh,
        in_specs=(
            P("radial", "mode", None, None),
            P("radial", "mode", None, None),
            P("mode", None, None),
            P("radial"),
        ),
        out_specs=P("radial", "mode", None, None),
        check_vma=False,
    )
```

profile of v0, /device:TPU:1, one launch (start us, length us, event | category | flops | bytes accessed | tf_op | source)
XLA Modules:
  0.0 699.8 jit_solution(18119201527040543334)
XLA Ops:
  6.5 2.0 convert_element_type.76
  8.5 5.2 fusion.40
  13.7 11.3 %copy.50 = bf16[32,16,2,768]{0,2,1,3:T(2,128)(2,1)} copy(bf16[32,16,2,768]{3,0,2,1:T(8,128)(2,1)S(1)} %fusion.40) | data formatting | bytes 3145728 | tf_op jit(solution)/shard_map/convert_element_type | solution.py:63
  25.0 8.3 %reshape.119 = bf16[4,2,98304]{2,1,0:T(2,128)(2,1)} reshape(bf16[768,16,2,32]{3,2,1,0:T(2,128)(2,1)} %bitcast.170) | data formatting | bytes 3145728
  33.3 5.5 all-to-all-start
  39.4 5.2 fusion.37
  44.6 11.3 %copy.54 = bf16[32,16,2,768]{0,2,1,3:T(2,128)(2,1)} copy(bf16[32,16,2,768]{3,0,2,1:T(8,128)(2,1)S(1)} %fusion.37) | data formatting | bytes 3145728 | tf_op jit(solution)/shard_map/convert_element_type | solution.py:69
  56.0 8.3 %reshape.121 = bf16[4,2,98304]{2,1,0:T(2,128)(2,1)} reshape(bf16[768,16,2,32]{3,2,1,0:T(2,128)(2,1)} %bitcast.171) | data formatting | bytes 3145728
  64.3 11.1 %all-to-all-done = bf16[4,2,98304]{2,1,0:T(2,128)(2,1)S(1)} async-done(((bf16[4,2,98304]{2,1,0:T(2,128)(2,1)}), bf16[4,2,98304]{2,1,0:T(2,128)(2,1)S(1)}, u32[]{:S(2)}, u32[]{:S(2)}) %all-to-all-start) | async-done | bytes 1572896 | tf_op jit(solution)/shard_map/all_to_all | solution.py:70
  75.4 4.5 all-to-all-start.1
  80.0 1.6 sine_negate_fusion
  81.6 4.7 reshape.120
  86.2 20.9 %copy.68 = bf16[32,16,2,4,192]{4,3,1,2,0:T(4,128)(2,1)} copy(bf16[32,16,2,4,192]{0,2,1,4,3:T(2,128)(2,1)} %bitcast.172) | data formatting | bytes 3145728 | tf_op jit(solution)/shard_map/all_to_all | solution.py:70
  107.1 2.1 copy.52
  109.2 7.2 %all-to-all-done.1 = bf16[4,2,98304]{2,1,0:T(2,128)(2,1)} async-done(((bf16[4,2,98304]{2,1,0:T(2,128)(2,1)}), bf16[4,2,98304]{2,1,0:T(2,128)(2,1)}, u32[]{:S(2)}, u32[]{:S(2)}) %all-to-all-start.1) | async-done | bytes 1572896 | tf_op jit(solution)/shard_map/all_to_all | solution.py:71
  116.4 6.4 reshape.122
  122.7 20.9 %copy.69 = bf16[32,16,2,4,192]{4,3,1,2,0:T(4,128)(2,1)} copy(bf16[32,16,2,4,192]{0,2,1,4,3:T(2,128)(2,1)} %bitcast.173) | data formatting | bytes 3145728 | tf_op jit(solution)/shard_map/all_to_all | solution.py:71
  143.6 3.4 copy.56
  147.0 14.8 %fusion.52 = f32[32,192,1536,1]{2,1,3,0:T(8,128)} fusion(bf16[32,64,2,192]{3,1,2,0:T(8,128)(2,1)S(1)} %bitcast.174, f32[64,1,1536]{2,0,1:T(8,128)S(1)} %get-tuple-element.644, f32[64,1,1536]{2,0,1:T(8,128)S(1)} %get-tuple-element.645), kind=kOutput, calls=%fused_computation.71 | convolution fusion | flops 2416508928 | bytes 40108032 | tf_op jit(solution)/shard_map/rmct,mcp->rtp/dot_general | solution.py:72
  161.7 17.3 %convert_bitcast_fusion = bf16[32,64,2,192]{3,1,0,2:T(8,128)(2,1)S(1)} fusion(f32[32,192,1536,1]{2,1,3,0:T(8,128)} %fusion.52, bf16[32,64,2,192]{3,1,2,0:T(8,128)(2,1)} %bitcast.179, f32[64,1,1536]{2,0,1:T(8,128)S(1)} %get-tuple-element.644, f32[64,1,1536]{2,0,1:T(8,128)S(1)} %get-tuple-element.645), kind=kOutput, calls=%fused_computation.54 | convolution fusion | flops 4852678656 | bytes 41680896 | tf_op jit(solution)/shard_map/rtp,mcp->rmct/dot_general | solution.py:79
  179.1 2.5 copy.57
  181.6 3.6 all-to-all-start.2
  185.5 47.4 %all-to-all-done.2 = bf16[32,64,2,192]{3,0,2,1:T(8,128)(2,1)S(1)} async-done(((bf16[32,64,2,192]{3,0,2,1:T(8,128)(2,1)}), bf16[32,64,2,192]{3,0,2,1:T(8,128)(2,1)S(1)}, u32[]{:S(2)}, u32[]{:S(2)}) %all-to-all-start.2) | async-done | bytes 1572896 | tf_op jit(solution)/shard_map/all_to_all | solution.py:82
  233.0 1.3 copy-done.1
  234.3 3.6 copy.86
  237.9 2.8 all_to_all.50
  240.7 7.6 %bitcast_add_fusion.1 = f32[32,16,2,384]{3,0,2,1:T(8,128)S(1)} fusion(f32[32,16,2,384]{3,2,1,0:T(2,128)} %param.14, bf16[32,16,2,768]{3,0,2,1:T(8,128)(2,1)} %all_to_all.50, bf16[16,384,768]{2,1,0:T(8,128)(2,1)} %param.16), kind=kOutput, calls=%fused_computation.57 | convolution fusion | flops 604372992 | bytes 14155776 | tf_op jit(solution)/shard_map/rmct,mjt->rmcj/dot_general | solution.py:83
  248.4 164.0 %while.77 = (s32[]{:T(128)}, f32[4,4,16,384]{3,2,1,0:T(8,128)S(1)}, s32[32]{0:T(128)S(1)}, f32[32]{0:T(128)S(1)}, f32[32,16,2,384]{3,0,2,1:T(8,128)S(1)}, /*inde...) while((s32[]{:T(128)}, f32[4,4,16,384]{3,2,1,0:T(8,128)S(1)}, ...), condition=%wide.region_2.3_spmd.clone, body=%wide.region_0.2_spmd.clone.sunk | while | flops 1161229 | bytes 2408801 | solution.py:121
  413.2 32.5 %all-gather.5.cloned.1.call-done = f32[32,4,16,384]{3,2,1,0:T(8,128)} async-done(((f32[4,4,16,384]{3,2,1,0:T(8,128)}), f32[32,4,16,384]{3,2,1,0:T(8,128)}) %all-gather.5.cloned.1.call-update) | async-done | bytes 3145744 | tf_op jit(solution)/shard_map/all_gather | solution.py:13
  445.8 9.0 %while.76 = (s32[]{:T(128)}, f32[4,4,16,384]{3,2,1,0:T(8,128)S(1)}, s32[]{:T(128)}, f32[8,4,4,16,384]{4,3,2,1,0:T(8,128)}, s32[]{:T(128)}) while((s32[]{:T(128)}, f32[4,4,16,384]{3,2,1,0:T(8,128)S(1)}, s32[]{:T(128)}, f32[8,4,4,16,384]{4,3,2,1,0:T(8,128)}, s32[]{:T(128)}) %tuple.172), condition=%wide.region_6.7_spmd, body=%wide.region_3.6_spmd.sunk | while | flops 1075203 | bytes 3588171 | solution.py:25
  445.8 1.0 dynamic-slice_bitcast_fusion.6
  447.1 1.0 dynamic-slice_bitcast_fusion.6
  448.4 1.0 dynamic-slice_bitcast_fusion.6
  449.7 1.0 dynamic-slice_bitcast_fusion.6
  450.9 1.0 dynamic-slice_bitcast_fusion.6
  452.2 1.0 dynamic-slice_bitcast_fusion.6
  453.5 1.0 dynamic-slice_bitcast_fusion.6
  455.2 1.9 broadcast.105.clone
  457.1 185.0 %while.78 = (s32[]{:T(128)}, f32[16,384]{1,0:T(8,128)S(1)}, f32[16,2,384]{2,1,0:T(2,128)S(1)}, f32[32,16,384]{2,1,0:T(8,128)S(1)}, f32[32,16,2,384]{3,2,1,0:T(2,...) while((s32[]{:T(128)}, f32[16,384]{1,0:T(8,128)S(1)}, ...), condition=%wide.region_8.9_spmd.clone, body=%wide.region_7.8_spmd.clone.sunk | while | flops 92172 | bytes 419129 | solution.py:136
  642.9 29.2 %while.79 = (s32[]{:T(128)}, f32[16,2,384]{2,1,0:T(2,128)S(1)}, f32[16,384]{1,0:T(8,128)S(1)}, f32[32,16,2,384]{3,2,1,0:T(2,128)S(1)}, f32[32,16,384]{2,1,0:T(8,...) while((s32[]{:T(128)}, f32[16,2,384]{2,1,0:T(2,128)S(1)}, ...), condition=%wide.region_10.11_spmd.clone, body=%wide.region_9.10_spmd.clone.sunk | while | flops 55300 | bytes 344196 | solution.py:149
  642.9 0.9 bitcast_dynamic-update-slice_fusion.11
  643.8 0.9 bitcast_dynamic-update-slice_fusion.11
  644.7 0.9 bitcast_dynamic-update-slice_fusion.11
  647.5 0.9 bitcast_dynamic-update-slice_fusion.11
  648.4 0.9 bitcast_dynamic-update-slice_fusion.11
  672.1 9.6 %all-gather.1 = f32[128,2,384]{2,1,0:T(2,128)S(1)} all-gather(f32[16,2,384]{2,1,0:T(2,128)S(1)} %get-tuple-element.408), channel_id=3, replica_groups=mesh['radial'=8,'mode'=4] {'radial'}, dimensions={0}, use_global_device_ids=true | all-gather | bytes 442368 | tf_op jit(solution)/shard_map/all_gather | solution.py:13
  681.8 8.3 %all-gather.2 = f32[128,384]{1,0:T(8,128)S(1)} all-gather(f32[16,384]{1,0:T(8,128)S(1)} %get-tuple-element.409), channel_id=4, replica_groups=mesh['radial'=8,'mode'=4] {'radial'}, dimensions={0}, use_global_device_ids=true | all-gather | bytes 221184 | tf_op jit(solution)/shard_map/all_gather | solution.py:13
  690.9 2.1 multiply_add_fusion.3
  (571 shorter events, 175.8 us)
Async XLA Ops:
  33.3 5.5 copy-start.2
  33.3 42.1 %all-to-all-start = ((bf16[4,2,98304]{2,1,0:T(2,128)(2,1)}), bf16[4,2,98304]{2,1,0:T(2,128)(2,1)S(1)}, u32[]{:S(2)}, u32[]{:S(2)}) async-start(bf16[4,2,98304]{2,1,0:T(2,128)(2,1)} %reshape.119), calls=%async_computation | async-start | bytes 3145728 | tf_op jit(solution)/shard_map/all_to_all | solution.py:70
  75.4 41.0 %all-to-all-start.1 = ((bf16[4,2,98304]{2,1,0:T(2,128)(2,1)}), bf16[4,2,98304]{2,1,0:T(2,128)(2,1)}, u32[]{:S(2)}, u32[]{:S(2)}) async-start(bf16[4,2,98304]{2,1,0:T(2,128)(2,1)} %reshape.121), calls=%async_computation.1 | async-start | bytes 3145728 | tf_op jit(solution)/shard_map/all_to_all | solution.py:71
  181.6 51.3 %all-to-all-start.2 = ((bf16[32,64,2,192]{3,0,2,1:T(8,128)(2,1)}), bf16[32,64,2,192]{3,0,2,1:T(8,128)(2,1)S(1)}, u32[]{:S(2)}, u32[]{:S(2)}) async-start(bf16[32,64,2,192]{3,0,2,1:T(8,128)(2,1)} %copy.57), calls=%async_computation.2 | async-start | bytes 4194304 | tf_op jit(solution)/shard_map/all_to_all | solution.py:82
  185.2 260.5 %all-gather.5.cloned.1.call-start = ((), (), s32[]{:S(2)}) async-start(), calls=%async_computation.3 | async-start | bytes 3538944 | tf_op jit(solution)/shard_map/all_gather | solution.py:13
  233.0 1.3 copy-start.1
  240.7 7.7 %copy-start.3 = (f32[32]{0:T(128)S(1)}, f32[32]{0:T(128)}, u32[]{:S(2)}) copy-start(f32[32]{0:T(128)} %param.17) | copy-start | bytes 388
  412.4 0.7 copy-start
Sparse Core Ops, SparseCore 0:
  413.3 32.4 all-gather.4
where the time goes:
time: 707 us; the launch traced here: 700 us
  loops' own time  204 us (29%)
  local copies, waits for them, and re-layouts  199 us (28%)
  other arithmetic  103 us (15%)
  waiting for transfers between devices  98.3 us (14%)
  matrix products  50.1 us (7%)
  blocking collectives  17.9 us (3%)
  starting transfers between devices  14 us (2%)
  between operations  13.7 us (2%)
    another operation x1, loops' own time, on_device(): lax.scan(sweep, (ratio_start, value_start), (diffusivity, right_side, glo...  102 us
    another operation x1, loops' own time, on_device(): lax.scan(compose, identity, (diffusivity, right_side, global_shells))  101 us
    dynamic_slice x224, local copies, waits for them, and re-layouts, on_device(): lax.scan(compose, identity, (diffusivity, right_side, global_shells))  79.9 us
    dynamic_update_slice x128, other arithmetic, on_device(): lax.scan(sweep, (ratio_start, value_start), (diffusivity, right_side, glo...  70.4 us
    all_to_all x1, waiting for transfers between devices, on_device(): lax.all_to_all(modes_grid, 'mode', split_axis=1, concat_axis=3, tiled=True)  47.4 us
    all_gather x1, waiting for transfers between devices, prefix_2(): pieces = jax.tree.map(lambda part: lax.all_gather(part, axis), value)  32.5 us
    unnamed x12, local copies, waits for them, and re-layouts  29.7 us
    all_to_all x2, local copies, waits for them, and re-layouts, on_device(): lax.all_to_all(flow_lat, 'mode', split_axis=3, concat_axis=1, tiled=True)  24.3 us
  transfers between devices with their start and end apart: 4, of which 4 were waited for; matrix products, arithmetic and copies ran while one was open for 8% of the time, Pallas kernels for 0%

commit v1 on v0

v1 whole, which is shorter than its diff:
```python
import functools
import math

import jax
import jax.numpy as jnp
import numpy as np
from jax import lax
from jax.experimental import pallas as pl
from jax.experimental.pallas import tpu as pltpu
from jax.sharding import PartitionSpec as P

NLON = 1536
VMEM_LIMIT = 60 * 1024 * 1024


def params(**more):
    return pltpu.CompilerParams(vmem_limit_bytes=VMEM_LIMIT, **more)


def grid_points(orders):
    needed = 3 * (orders - 1) + 1
    return next(q for q in range(128, NLON + 1, 128) if q >= needed and NLON % q == 0)


def longitude_tables(orders):
    points = grid_points(orders)
    stride = NLON // points
    phase = np.arange(orders)[:, None] * (np.arange(points) * stride)[None, :] % NLON
    angle = phase.astype(np.float32) * np.float32(2.0 * math.pi / NLON)
    paired = np.stack([np.cos(angle), -np.sin(angle)], axis=1).reshape(2 * orders, points)
    synth = (paired / np.float32(math.sqrt(orders))).astype(jnp.bfloat16)
    analysis = (paired * np.float32(math.sqrt(2.0 / NLON))).astype(jnp.bfloat16)
    return jnp.asarray(synth.T), jnp.asarray(analysis), float(stride)


def to_latitudes(parts, field_ref, flow_ref, table_ref, out_ref, rows_ref):
    order = pl.program_id(0)
    shells = field_ref.shape[0]
    lanes = rows_ref.shape[0]
    count = 4 * shells
    stacked = jnp.concatenate(
        [ref[:, 0, half, :] for half in range(2) for ref in (field_ref, flow_ref)], axis=0
    ).astype(jnp.bfloat16)
    lat = jnp.dot(stacked, table_ref[0], preferred_element_type=jnp.float32)
    base = pl.multiple_of(order * count, count)
    for lane in range(lanes):
        rows_ref[lane, pl.ds(base, count), :] = lat[:, lane * 128 : (lane + 1) * 128]

    @pl.when(order == pl.num_programs(0) - 1)
    def _():
        mine = shells // parts
        modes = rows_ref.shape[1] // (2 * shells)
        for part in range(parts):
            for which in range(2):
                for shell in range(mine):
                    start = which * shells + part * mine + shell
                    for lane in range(lanes):
                        picked = rows_ref[lane, pl.ds(start, modes, stride=2 * shells), :]
                        out_ref[part, which, shell, :, lane * 128 : (lane + 1) * 128] = (
                            picked.astype(jnp.bfloat16)
                        )


def through_grid(scale, lat_ref, synth_ref, analysis_ref, out_ref):
    parts, _, _, modes, _ = lat_ref.shape
    grids = []
    for which in range(2):
        lat = jnp.concatenate([lat_ref[part, which, 0] for part in range(parts)], axis=0)
        grids.append(jnp.dot(synth_ref[...], lat, preferred_element_type=jnp.float32))
    product = (grids[0] * grids[1]).astype(jnp.bfloat16)
    back = jnp.dot(analysis_ref[...], product, preferred_element_type=jnp.float32) * scale
    for part in range(parts):
        out_ref[part, 0] = back[part * modes : (part + 1) * modes].astype(jnp.bfloat16)


def eliminate(
    nr_total, where_ref, kappa_ref, back_ref, table_ref, field_ref,
    alpha_ref, beta_ref, gamma_ref, edge_ref, wide_ref, right_ref,
):
    order = pl.program_id(0)
    shells, modes, _ = back_ref.shape
    ord_dev = modes // 2
    degrees = field_ref.shape[3]
    lanes = wide_ref.shape[0]
    blocks = right_ref.shape[0]

    @pl.when(order == 0)
    def _():
        for shell in range(shells):
            for lane in range(lanes):
                wide_ref[lane, shell * modes : (shell + 1) * modes, :] = back_ref[
                    shell, :, lane * 128 : (lane + 1) * 128
                ].astype(jnp.float32)

    picked = jnp.concatenate(
        [
            jnp.concatenate(
                [
                    wide_ref[lane, pl.ds(2 * order + half, shells, stride=modes), :].astype(jnp.bfloat16)
                    for lane in range(lanes)
                ],
                axis=1,
            )
            for half in range(2)
        ],
        axis=0,
    )
    forcing = lax.dot_general(
        picked, table_ref[0], (((1,), (1,)), ((), ())), preferred_element_type=jnp.float32
    )
    for half in range(2):
        right = field_ref[:, 0, half, :] + forcing[half * shells : (half + 1) * shells]
        for block in range(blocks):
            right_ref[block, pl.ds(half * ord_dev + order, shells, stride=modes), :] = right[
                :, block * 128 : (block + 1) * 128
            ]

    @pl.when(order == pl.num_programs(0) - 1)
    def _():
        first = where_ref[0] * shells
        first_order = where_ref[1] * ord_dev
        offset = nr_total * 7 // 13
        for block in range(blocks):
            at = slice(block * 128, (block + 1) * 128)
            degree = (
                first_order
                + block * 128
                + lax.broadcasted_iota(jnp.int32, (ord_dev, 128), 0)
                + lax.broadcasted_iota(jnp.int32, (ord_dev, 128), 1)
            ).astype(jnp.float32)
            angular = degree * (degree + 1.0)

            def forward(shell, carry):
                ratio, value0, value1, pull = carry
                index = first + shell
                kappa = kappa_ref[shell]
                lower = jnp.where(index > 0, -kappa, 0.0)
                upper = jnp.where(index < nr_total - 1, -kappa, 0.0)
                radius = jnp.full((ord_dev, 128), offset + index, jnp.int32).astype(jnp.float32)
                diagonal = 1.0 + 2.0 * kappa + kappa * angular / (radius * radius)
                inverse = 1.0 / (diagonal - lower * ratio)
                start = pl.multiple_of(shell * modes, modes)
                ratio = upper * inverse
                value0 = (right_ref[block, pl.ds(start, ord_dev), :] - lower * value0) * inverse
                value1 = (
                    right_ref[block, pl.ds(start + ord_dev, ord_dev), :] - lower * value1
                ) * inverse
                pull = -lower * pull * inverse
                alpha_ref[shell, :ord_dev, at] = value0
                alpha_ref[shell, ord_dev:, at] = value1
                beta_ref[shell, :, at] = pull
                gamma_ref[shell, :, at] = ratio
                return ratio, value0, value1, pull

            blank = jnp.zeros((ord_dev, 128), jnp.float32)
            unity = jnp.ones((ord_dev, 128), jnp.float32)
            lax.fori_loop(0, shells, forward, (blank, blank, blank, unity), unroll=4)

            def backward(step, carry):
                alpha0, alpha1, beta, gamma = carry
                shell = shells - 1 - step
                ratio = gamma_ref[shell, :, at]
                alpha0 = alpha_ref[shell, :ord_dev, at] - ratio * alpha0
                alpha1 = alpha_ref[shell, ord_dev:, at] - ratio * alpha1
                beta = beta_ref[shell, :, at] - ratio * beta
                gamma = -ratio * gamma
                alpha_ref[shell, :ord_dev, at] = alpha0
                alpha_ref[shell, ord_dev:, at] = alpha1
                beta_ref[shell, :, at] = beta
                gamma_ref[shell, :, at] = gamma
                return alpha0, alpha1, beta, gamma

            lax.fori_loop(0, shells, backward, (blank, blank, blank, unity), unroll=4)
            for side, shell in enumerate((0, shells - 1)):
                edge_ref[4 * side, :, at] = alpha_ref[shell, :ord_dev, at]
                edge_ref[4 * side + 1, :, at] = alpha_ref[shell, ord_dev:, at]
                edge_ref[4 * side + 2, :, at] = beta_ref[shell, :, at]
                edge_ref[4 * side + 3, :, at] = gamma_ref[shell, :, at]


def finish(where_ref, edges_ref, alpha_ref, beta_ref, gamma_ref, out_ref):
    count = edges_ref.shape[0]
    shells, modes, degrees = alpha_ref.shape
    ord_dev = modes // 2
    mine = where_ref[0]
    for block in range(degrees // 128):
        at = slice(block * 128, (block + 1) * 128)
        blank = jnp.zeros((ord_dev, 128), jnp.float32)
        known = [blank, blank]
        slope = blank
        lefts, firsts = [], []
        for device in range(count):
            head = [edges_ref[device, k, :, at] for k in range(4)]
            tail = [edges_ref[device, 4 + k, :, at] for k in range(4)]
            lefts.append((known, slope))
            inverse = 1.0 / (1.0 - head[2] * slope)
            const = [(head[c] + head[2] * known[c]) * inverse for c in range(2)]
            gain = head[3] * inverse
            firsts.append((const, gain))
            known = [tail[c] + tail[2] * (known[c] + slope * const[c]) for c in range(2)]
            slope = tail[3] + tail[2] * slope * gain
        beyond = [blank, blank]
        before = [blank, blank]
        after = [blank, blank]
        for device in reversed(range(count)):
            const, gain = firsts[device]
            left, tilt = lefts[device]
            here = mine == device
            start = [const[c] + gain * beyond[c] for c in range(2)]
            before = [jnp.where(here, left[c] + tilt * start[c], before[c]) for c in range(2)]
            after = [jnp.where(here, beyond[c], after[c]) for c in range(2)]
            beyond = start

        def emit(shell, carry):
            beta, gamma = beta_ref[shell, :, at], gamma_ref[shell, :, at]
            for half in range(2):
                out_ref[shell, :, half, at] = (
                    alpha_ref[shell, half * ord_dev : (half + 1) * ord_dev, at]
                    + beta * before[half]
                    + gamma * after[half]
                )
            return carry

        lax.fori_loop(0, shells, emit, 0, unroll=4)


def on_device(scalar_field, radial_flow, legendre, diffusivity):
    shells, ord_dev, _, degrees = scalar_field.shape
    lats = legendre.shape[2]
    parts, rings = lax.axis_size("mode"), lax.axis_size("radial")
    orders = ord_dev * parts
    modes = 2 * ord_dev
    mine = shells // parts
    synth, analysis, scale = longitude_tables(orders)
    points = synth.shape[0]
    where = jnp.stack([lax.axis_index("radial"), lax.axis_index("mode")]).astype(jnp.int32)

    spectral = pl.BlockSpec((shells, 1, 2, degrees), lambda m: (0, m, 0, 0))
    table = pl.BlockSpec((1, degrees, lats), lambda m: (m, 0, 0))
    smem = pl.BlockSpec(memory_space=pltpu.SMEM)

    def whole(*shape):
        return pl.BlockSpec(shape, lambda *_: (0,) * len(shape))

    lat = pl.pallas_call(
        functools.partial(to_latitudes, parts),
        grid=(ord_dev,),
        in_specs=[spectral, spectral, table],
        out_specs=whole(parts, 2, mine, modes, lats),
        out_shape=jax.ShapeDtypeStruct((parts, 2, mine, modes, lats), jnp.bfloat16),
        scratch_shapes=[pltpu.VMEM((lats // 128, 4 * shells * ord_dev, 128), jnp.float32)],
        compiler_params=params(),
        name="to_latitudes",
    )(scalar_field, radial_flow, legendre)
    lat = lax.all_to_all(lat, "mode", split_axis=0, concat_axis=0, tiled=True)
    back = pl.pallas_call(
        functools.partial(through_grid, scale),
        grid=(mine,),
        in_specs=[
            pl.BlockSpec((parts, 2, 1, modes, lats), lambda r: (0, 0, r, 0, 0)),
            whole(points, 2 * orders),
            whole(2 * orders, points),
        ],
        out_specs=pl.BlockSpec((parts, 1, modes, lats), lambda r: (0, r, 0, 0)),
        out_shape=jax.ShapeDtypeStruct((parts, mine, modes, lats), jnp.bfloat16),
        compiler_params=params(),
        name="through_grid",
    )(lat, synth, analysis)
    back = lax.all_to_all(back, "mode", split_axis=0, concat_axis=0, tiled=True)
    back = back.reshape(shells, modes, lats)
    f32 = jnp.float32
    alpha, beta, gamma, edge = pl.pallas_call(
        functools.partial(eliminate, shells * rings),
        grid=(ord_dev,),
        in_specs=[smem, smem, whole(shells, modes, lats), table, spectral],
        out_specs=[
            whole(shells, modes, degrees),
            whole(shells, ord_dev, degrees),
            whole(shells, ord_dev, degrees),
            whole(8, ord_dev, degrees),
        ],
        out_shape=[
            jax.ShapeDtypeStruct((shells, modes, degrees), f32),
            jax.ShapeDtypeStruct((shells, ord_dev, degrees), f32),
            jax.ShapeDtypeStruct((shells, ord_dev, degrees), f32),
            jax.ShapeDtypeStruct((8, ord_dev, degrees), f32),
        ],
        scratch_shapes=[
            pltpu.VMEM((lats // 128, shells * modes, 128), f32),
            pltpu.VMEM((degrees // 128, shells * modes, 128), f32),
        ],
        compiler_params=params(),
        name="eliminate",
    )(where, diffusivity, back, legendre, scalar_field)
    edges = lax.all_gather(edge, "radial")
    return pl.pallas_call(
        finish,
        in_specs=[smem] + [pl.BlockSpec(memory_space=pltpu.VMEM)] * 4,
        out_specs=pl.BlockSpec(memory_space=pltpu.VMEM),
        out_shape=jax.ShapeDtypeStruct(scalar_field.shape, f32),
        compiler_params=params(),
        name="finish",
    )(where, edges, alpha, beta, gamma)


def solution(mesh):
    return jax.shard_map(
        on_device,
        mesh=mesh,
        in_specs=(
            P("radial", "mode", None, None),
            P("radial", "mode", None, None),
            P("mode", None, None),
            P("radial"),
        ),
        out_specs=P("radial", "mode", None, None),
        check_vma=False,
    )
```

time: 707 us -> 206 us (0.29)
  loops' own time: 204 us -> 0 us
  local copies, waits for them, and re-layouts: 199 us -> 1.14 us
  other arithmetic: 103 us -> 0.58 us
  blocking collectives: 17.9 us -> 76.5 us
  matrix products: 50.1 us -> 0 us
  Pallas kernels: 0 us -> 48.6 us
  waiting for transfers between devices: 98.3 us -> 61.3 us
  starting transfers between devices: 14 us -> 3.6 us
    another operation x5 -> x0, loops' own time: 204 us -> none  [the longest x1 102 us: on_device(): lax.scan(sweep, (ratio_start, value_start), (diffusivity, right_side, glo...]
    dynamic_slice x224 -> x0, local copies, waits for them, and re-layouts: 79.9 us -> none  [on_device(): lax.scan(compose, identity, (diffusivity, right_side, global_shells))]
    all_to_all x0 -> x1, blocking collectives: none -> 76.5 us  [on_device(): lat = lax.all_to_all(lat, 'mode', split_axis=0, concat_axis=0, tiled=True)]
    dynamic_update_slice x128 -> x0, other arithmetic: 70.4 us -> none  [on_device(): lax.scan(sweep, (ratio_start, value_start), (diffusivity, right_side, glo...]
    all_to_all x6 -> x0, local copies, waits for them, and re-layouts: 53.6 us -> none  [the longest x2 24.3 us: on_device(): lax.all_to_all(flow_lat, 'mode', split_axis=3, concat_axis=1, tiled=True)]
    dot_general x5 -> x0, matrix products: 50.1 us -> none  [the longest x1 17.3 us: on_device(): jnp.einsum('rtp,mcp->rmct', product, analysis_table, preferred_element_ty...]
    pallas_call x0 -> x4, Pallas kernels: none -> 48.6 us  [the longest x1 19.1 us: on_device(): pl.pallas_call(functools.partial(to_latitudes, parts), grid=(ord_dev,), i...]
    all_to_all x3 -> x1, waiting for transfers between devices: 65.7 us -> 35.9 us  [on_device(): back = lax.all_to_all(back, 'mode', split_axis=0, concat_axis=0, tiled=True)]
  transfers between devices with their start and end apart: 4 -> 2, of which waited for: 4 -> 2; matrix products, arithmetic and copies ran while one was open for 8% -> 0% of each run, Pallas kernels for 0% -> 0%
where the time goes in v1:
time: 206 us; the launch traced here: 205 us
  blocking collectives  76.5 us (37%)
  waiting for transfers between devices  61.3 us (30%)
  Pallas kernels  48.6 us (24%)
  between operations  13.4 us (7%)
  starting transfers between devices  3.6 us (2%)
    all_to_all x1, blocking collectives, on_device(): lat = lax.all_to_all(lat, 'mode', split_axis=0, concat_axis=0, tiled=True)  76.5 us
    all_to_all x1, waiting for transfers between devices, on_device(): back = lax.all_to_all(back, 'mode', split_axis=0, concat_axis=0, tiled=True)  35.9 us
    all_gather x1, waiting for transfers between devices, on_device(): edges = lax.all_gather(edge, 'radial')  25.4 us
    pallas_call x1, Pallas kernels, on_device(): pl.pallas_call(functools.partial(to_latitudes, parts), grid=(ord_dev,), i...  19.1 us
    pallas_call x1, Pallas kernels, on_device(): pl.pallas_call(functools.partial(eliminate, shells * rings), grid=(ord_de...  16.9 us
    pallas_call x1, Pallas kernels, on_device(): pl.pallas_call(functools.partial(through_grid, scale), grid=(mine,), in_s...  7.73 us
    pallas_call x1, Pallas kernels, on_device(): pl.pallas_call(finish, in_specs=[smem] + [pl.BlockSpec(memory_space=pltpu...  4.96 us
  transfers between devices with their start and end apart: 2, of which 2 were waited for; matrix products, arithmetic and copies ran while one was open for 0% of the time, Pallas kernels for 0%

profile of v1, /device:TPU:1, one launch (start us, length us, event | category | flops | bytes accessed | tf_op | source)
XLA Modules:
  0.0 205.2 jit_solution(1972605678271524005)
XLA Ops:
  6.5 19.1 %to_latitudes.1 = bf16[4,2,8,32,768]{4,3,2,1,0:T(8,128)(2,1)} custom-call(f32[32,16,2,384]{3,2,1,0:T(2,128)} %field_ref.3, f32[32,16,2,384]{3,2,1,0:T(2,128)} %flow_ref.1, bf16[16,384,768]{2,1,0:T(8,128)(2,1)} %table_ref.3), custom_call_target="tpu_custom_call" | custom-call | tf_op jit(solution)/shard_map/to_latitudes/pallas_call | solution.py:245
  25.6 76.5 %all_to_all.10.lat_ref = bf16[4,2,8,32,768]{4,3,2,1,0:T(8,128)(2,1)} all-to-all(bf16[4,2,8,32,768]{4,3,2,1,0:T(8,128)(2,1)} %to_latitudes.1), channel_id=1, replica_groups=mesh['radial'=8,'mode'=4] {'mode'}, dimensions={0} | all-to-all | bytes 6291456 | tf_op jit(solution)/shard_map/all_to_all | solution.py:255
  102.1 7.7 %through_grid.1 = bf16[4,8,32,768]{3,2,1,0:T(8,128)(2,1)} custom-call(bf16[4,2,8,32,768]{4,3,2,1,0:T(8,128)(2,1)} %all_to_all.10.lat_ref, bf16[256,128]{1,0:T(8,128)(2,1)} %constant.13.clone.synth_ref, bf16[128,256]{1,0:T(8,128)(2,1)} %constant.14.clone.analysis_ref), custom_call_target="tpu_custom_call" | custom-call | tf_op jit(solution)/shard_map/through_grid/pallas_call | solution.py:256
  109.8 3.6 %all-to-all-start.1 = ((bf16[4,8,32,768]{3,2,1,0:T(8,128)(2,1)}), bf16[4,8,32,768]{3,2,1,0:T(8,128)(2,1)S(1)}, u32[]{:S(2)}, u32[]{:S(2)}) async-start(bf16[4,8,32,768]{3,2,1,0:T(8,128)(2,1)} %through_grid.1), calls=%async_computation.1 | async-start | bytes 3145728 | tf_op jit(solution)/shard_map/all_to_all | solution.py:269
  113.4 0.0 all-gather.3.cloned.1.call-start
  113.5 0.6 pad_add_fusion.where_ref
  114.0 35.9 %all-to-all-done.1 = bf16[4,8,32,768]{3,2,1,0:T(8,128)(2,1)S(1)} async-done(((bf16[4,8,32,768]{3,2,1,0:T(8,128)(2,1)}), bf16[4,8,32,768]{3,2,1,0:T(8,128)(2,1)S(1)}, u32[]{:S(2)}, u32[]{:S(2)}) %all-to-all-start.1) | async-done | bytes 1572896 | tf_op jit(solution)/shard_map/all_to_all | solution.py:269
  149.9 0.0 copy-start
  149.9 1.1 copy-done
  151.0 16.9 %eliminate.1 = (f32[32,32,384]{2,1,0:T(8,128)}, f32[32,16,384]{2,1,0:T(8,128)}, f32[32,16,384]{2,1,0:T(8,128)}, f32[8,16,384]{2,1,0:T(8,128)}) custom-call(s32[2]{0:T(128)} %pad_add_fusion.where_ref, f32[32]{0:T(128)} %kappa_ref.1, bf16[32,32,768]{2,1,0:T(8,128)(2,1)} %bitcast.4, bf16[16,384,768]{2,1,0:T(8,128)(2,1)} %table_ref.3, f32[32,16,2,384]{3,2,1,0:T(2,128)} %field_ref.3), custom_call_target="tpu_custom_call" | custom-call | tf_op jit(solution)/shard_map/eliminate/pallas_call | solution.py:272
  167.9 0.0 all-gather.3.cloned.1.call-update
  167.9 25.4 %all-gather.3.cloned.1.call-done = f32[64,16,384]{2,1,0:T(8,128)} async-done(((f32[8,16,384]{2,1,0:T(8,128)}), f32[64,16,384]{2,1,0:T(8,128)}) %all-gather.3.cloned.1.call-update) | async-done | bytes 1572880 | tf_op jit(solution)/shard_map/all_gather | solution.py:295
  193.4 5.0 %finish.1 = f32[32,16,2,384]{3,2,1,0:T(2,128)} custom-call(s32[2]{0:T(128)} %pad_add_fusion.where_ref, f32[8,8,16,384]{3,2,1,0:T(8,128)} %bitcast.5, f32[32,32,384]{2,1,0:T(8,128)} %get-tuple-element.10.alpha_ref, f32[32,16,384]{2,1,0:T(8,128)} %get-tuple-element.11.beta_ref, f32[32,16,384]{2,1,0:T(8,128)} %get-tuple-element.12.gamma_ref), custom_call_target="tpu_custom_call" | custom-call | tf_op jit(solution)/shard_map/finish/pallas_call | solution.py:296
Async XLA Ops:
  109.8 40.1 %all-to-all-start.1 = ((bf16[4,8,32,768]{3,2,1,0:T(8,128)(2,1)}), bf16[4,8,32,768]{3,2,1,0:T(8,128)(2,1)S(1)}, u32[]{:S(2)}, u32[]{:S(2)}) async-start(bf16[4,8,32,768]{3,2,1,0:T(8,128)(2,1)} %through_grid.1), calls=%async_computation.1 | async-start | bytes 3145728 | tf_op jit(solution)/shard_map/all_to_all | solution.py:269
  113.4 80.0 %all-gather.3.cloned.1.call-start = ((), (), s32[]{:S(2)}) async-start(), calls=%async_computation.2 | async-start | bytes 1769472 | tf_op jit(solution)/shard_map/all_gather | solution.py:295
  149.9 1.1 copy-start
Sparse Core Ops, SparseCore 0:
  168.1 25.2 all-gather.2

commit v2 on v0

v2 whole, which is shorter than its diff:
```python
import functools
import math

import jax
import jax.numpy as jnp
import numpy as np
from jax import lax
from jax.experimental import pallas as pl
from jax.experimental.pallas import tpu as pltpu
from jax.sharding import PartitionSpec as P

NLON = 1536
VMEM_LIMIT = 60 * 1024 * 1024


def params(**more):
    return pltpu.CompilerParams(vmem_limit_bytes=VMEM_LIMIT, **more)


def grid_points(orders):
    needed = 3 * (orders - 1) + 1
    return next(q for q in range(128, NLON + 1, 128) if q >= needed and NLON % q == 0)


def longitude_tables(orders):
    points = grid_points(orders)
    stride = NLON // points
    phase = np.arange(orders)[:, None] * (np.arange(points) * stride)[None, :] % NLON
    angle = phase.astype(np.float32) * np.float32(2.0 * math.pi / NLON)
    paired = np.stack([np.cos(angle), -np.sin(angle)], axis=1).reshape(2 * orders, points)
    synth = (paired / np.float32(math.sqrt(orders))).astype(jnp.bfloat16)
    analysis = (paired * np.float32(math.sqrt(2.0 / NLON))).astype(jnp.bfloat16)
    return jnp.asarray(synth.T), jnp.asarray(analysis), float(stride)


def whole_step(
    chunks, scale, kappa_ref, table_hbm, field_ref, flow_ref, synth_ref, analysis_ref, out_ref,
    table_ref, spectral_ref, rows_ref, send_ref, recv_ref, back_send_ref, back_recv_ref,
    wide_ref, sum_ref, right_ref, alpha_ref, beta_ref, gamma_ref, edge_ref, edges_ref,
    table_sem, send_sem, recv_sem, back_send_sem, back_recv_sem, edge_send_sem, edge_recv_sem,
):
    shells, ord_dev, _, degrees = field_ref.shape
    modes = 2 * ord_dev
    parts, rings = lax.axis_size("mode"), lax.axis_size("radial")
    me, ring = lax.axis_index("mode"), lax.axis_index("radial")
    mine = shells // parts
    count = 4 * shells
    width = table_ref.shape[3]
    lanes, blocks = width // 128, degrees // 128
    nr_total = shells * rings

    def table_copy(chunk):
        return pltpu.make_async_copy(
            table_hbm.at[:, :, pl.ds(chunk * width, width)], table_ref.at[chunk], table_sem.at[chunk]
        )

    for chunk in range(chunks):
        table_copy(chunk).start()

    barrier = pltpu.get_barrier_semaphore()
    for hop in range(1, parts):
        pl.semaphore_signal(
            barrier, inc=1, device_id={"mode": lax.rem(me + hop, parts)},
            device_id_type=pl.DeviceIdType.MESH,
        )
    for hop in range(1, rings):
        pl.semaphore_signal(
            barrier, inc=1, device_id={"radial": lax.rem(ring + hop, rings)},
            device_id_type=pl.DeviceIdType.MESH,
        )

    def exchange(axis, hop, source, target, send, receive):
        here, size = (me, parts) if axis == "mode" else (ring, rings)
        return pltpu.make_async_remote_copy(
            src_ref=source, dst_ref=target, send_sem=send, recv_sem=receive,
            device_id={axis: lax.rem(here + hop, size)}, device_id_type=pl.DeviceIdType.MESH,
        )

    def lat_copy(chunk, hop, slot):
        to = lax.rem(me + hop, parts)
        return exchange(
            "mode", hop, send_ref.at[chunk, to], recv_ref.at[chunk, slot],
            send_sem.at[chunk, hop - 1], recv_sem.at[chunk, hop - 1],
        )

    def back_copy(chunk, hop, slot):
        to = lax.rem(me + hop, parts)
        return exchange(
            "mode", hop, back_send_ref.at[chunk, to], back_recv_ref.at[chunk, slot],
            back_send_sem.at[chunk, hop - 1], back_recv_sem.at[chunk, hop - 1],
        )

    def edge_copy(hop, slot):
        return exchange(
            "radial", hop, edge_ref, edges_ref.at[slot],
            edge_send_sem.at[hop - 1], edge_recv_sem.at[hop - 1],
        )

    def stack(order, carry):
        spectral_ref[order] = jnp.concatenate(
            [ref[:, order, half, :] for half in range(2) for ref in (field_ref, flow_ref)], axis=0
        ).astype(jnp.bfloat16)
        return carry

    lax.fori_loop(0, ord_dev, stack, 0, unroll=2)

    for chunk in range(chunks):
        table_copy(chunk).wait()

        def transform(order, carry):
            lat = jnp.dot(
                spectral_ref[order], table_ref[chunk, order], preferred_element_type=jnp.float32
            )
            base = pl.multiple_of(order * count, count)
            for lane in range(lanes):
                rows_ref[lane, pl.ds(base, count), :] = lat[:, lane * 128 : (lane + 1) * 128]
            return carry

        lax.fori_loop(0, ord_dev, transform, 0, unroll=2)

        def pack(row, carry):
            which, shell = row // shells, row % shells
            part, local = shell // mine, shell % mine
            for lane in range(lanes):
                picked = rows_ref[lane, pl.ds(row, modes, stride=2 * shells), :]
                send_ref[chunk, part, which, local, :, lane * 128 : (lane + 1) * 128] = (
                    picked.astype(jnp.bfloat16)
                )
            return carry

        lax.fori_loop(0, 2 * shells, pack, 0, unroll=4)
        recv_ref[chunk, me] = send_ref[chunk, me]
        if chunk == 0:
            pl.semaphore_wait(barrier, parts + rings - 2)
        for hop in range(1, parts):
            lat_copy(chunk, hop, me).start()

    for chunk in range(chunks):
        for hop in range(1, parts):
            lat_copy(chunk, hop, lax.rem(me + parts - hop, parts)).wait_recv()

        def multiply(local, carry):
            grids = []
            for which in range(2):
                lat = jnp.concatenate(
                    [recv_ref[chunk, part, which, local] for part in range(parts)], axis=0
                )
                grids.append(jnp.dot(synth_ref[...], lat, preferred_element_type=jnp.float32))
            product = (grids[0] * grids[1]).astype(jnp.bfloat16)
            back = jnp.dot(analysis_ref[...], product, preferred_element_type=jnp.float32) * scale
            for part in range(parts):
                back_send_ref[chunk, part, local] = back[part * modes : (part + 1) * modes].astype(
                    jnp.bfloat16
                )
            return carry

        lax.fori_loop(0, mine, multiply, 0)
        back_recv_ref[chunk, me] = back_send_ref[chunk, me]
        for hop in range(1, parts):
            back_copy(chunk, hop, me).start()

    for chunk in range(chunks):
        for hop in range(1, parts):
            back_copy(chunk, hop, lax.rem(me + parts - hop, parts)).wait_recv()

        def widen(shell, carry):
            base = pl.multiple_of(shell * modes, modes)
            for lane in range(lanes):
                wide_ref[lane, pl.ds(base, modes), :] = back_recv_ref[
                    chunk, shell // mine, shell % mine, :, lane * 128 : (lane + 1) * 128
                ].astype(jnp.float32)
            return carry

        lax.fori_loop(0, shells, widen, 0, unroll=4)

        def untransform(order, carry):
            picked = jnp.concatenate(
                [
                    jnp.concatenate(
                        [
                            wide_ref[lane, pl.ds(2 * order + half, shells, stride=modes), :].astype(
                                jnp.bfloat16
                            )
                            for lane in range(lanes)
                        ],
                        axis=1,
                    )
                    for half in range(2)
                ],
                axis=0,
            )
            forcing = lax.dot_general(
                picked, table_ref[chunk, order], (((1,), (1,)), ((), ())),
                preferred_element_type=jnp.float32,
            )
            if chunk > 0:
                forcing = sum_ref[order] + forcing
            if chunk < chunks - 1:
                sum_ref[order] = forcing
                return carry
            for half in range(2):
                right = field_ref[:, order, half, :] + forcing[half * shells : (half + 1) * shells]
                for block in range(blocks):
                    right_ref[block, pl.ds(half * ord_dev + order, shells, stride=modes), :] = right[
                        :, block * 128 : (block + 1) * 128
                    ]
            return carry

        lax.fori_loop(0, ord_dev, untransform, 0, unroll=2)

    offset = nr_total * 7 // 13
    cut = [slice(block * 128, (block + 1) * 128) for block in range(blocks)]
    tile = (ord_dev, 128)
    angulars = []
    for block in range(blocks):
        degree = (
            me * ord_dev
            + block * 128
            + lax.broadcasted_iota(jnp.int32, tile, 0)
            + lax.broadcasted_iota(jnp.int32, tile, 1)
        ).astype(jnp.float32)
        angulars.append(degree * (degree + 1.0))

    def forward(shell, carry):
        index = ring * shells + shell
        kappa = jnp.full(tile, kappa_ref[shell], jnp.float32)
        spot = jnp.full(tile, index, jnp.int32)
        lower = jnp.where(spot > 0, -kappa, 0.0)
        upper = jnp.where(spot < nr_total - 1, -kappa, 0.0)
        radius = (offset + spot).astype(jnp.float32)
        weight = kappa / (radius * radius)
        start = pl.multiple_of(shell * modes, modes)
        new = []
        for block in range(blocks):
            ratio, value0, value1, pull = carry[block]
            diagonal = 1.0 + 2.0 * kappa + weight * angulars[block]
            inverse = 1.0 / (diagonal - lower * ratio)
            ratio = upper * inverse
            value0 = (right_ref[block, pl.ds(start, ord_dev), :] - lower * value0) * inverse
            value1 = (
                right_ref[block, pl.ds(start + ord_dev, ord_dev), :] - lower * value1
            ) * inverse
            pull = -lower * pull * inverse
            alpha_ref[shell, :ord_dev, cut[block]] = value0
            alpha_ref[shell, ord_dev:, cut[block]] = value1
            beta_ref[shell, :, cut[block]] = pull
            gamma_ref[shell, :, cut[block]] = ratio
            new.append((ratio, value0, value1, pull))
        return tuple(new)

    blank = jnp.zeros(tile, jnp.float32)
    unity = jnp.ones(tile, jnp.float32)
    outset = tuple((blank, blank, blank, unity) for _ in range(blocks))
    lax.fori_loop(0, shells, forward, outset)

    def backward(step, carry):
        shell = shells - 1 - step
        new = []
        for block in range(blocks):
            alpha0, alpha1, beta, gamma = carry[block]
            ratio = gamma_ref[shell, :, cut[block]]
            alpha0 = alpha_ref[shell, :ord_dev, cut[block]] - ratio * alpha0
            alpha1 = alpha_ref[shell, ord_dev:, cut[block]] - ratio * alpha1
            beta = beta_ref[shell, :, cut[block]] - ratio * beta
            gamma = -ratio * gamma
            alpha_ref[shell, :ord_dev, cut[block]] = alpha0
            alpha_ref[shell, ord_dev:, cut[block]] = alpha1
            beta_ref[shell, :, cut[block]] = beta
            gamma_ref[shell, :, cut[block]] = gamma
            new.append((alpha0, alpha1, beta, gamma))
        return tuple(new)

    lax.fori_loop(0, shells, backward, outset)

    for side, shell in enumerate((0, shells - 1)):
        edge_ref[4 * side] = alpha_ref[shell, :ord_dev]
        edge_ref[4 * side + 1] = alpha_ref[shell, ord_dev:]
        edge_ref[4 * side + 2] = beta_ref[shell]
        edge_ref[4 * side + 3] = gamma_ref[shell]
    edges_ref[ring] = edge_ref[...]
    for hop in range(1, rings):
        edge_copy(hop, ring).start()
    for hop in range(1, rings):
        edge_copy(hop, lax.rem(ring + rings - hop, rings)).wait_recv()

    spot = jnp.full(tile, ring, jnp.int32)
    for block in range(blocks):
        known, slope = [blank, blank], blank
        lefts, firsts = [], []
        for device in range(rings):
            head = [edges_ref[device, k, :, cut[block]] for k in range(4)]
            tail = [edges_ref[device, 4 + k, :, cut[block]] for k in range(4)]
            lefts.append((known, slope))
            inverse = 1.0 / (1.0 - head[2] * slope)
            const = [(head[c] + head[2] * known[c]) * inverse for c in range(2)]
            gain = head[3] * inverse
            firsts.append((const, gain))
            known = [tail[c] + tail[2] * (known[c] + slope * const[c]) for c in range(2)]
            slope = tail[3] + tail[2] * slope * gain
        beyond, before, after = [blank, blank], [blank, blank], [blank, blank]
        for device in reversed(range(rings)):
            const, gain = firsts[device]
            left, tilt = lefts[device]
            here = spot == device
            start = [const[c] + gain * beyond[c] for c in range(2)]
            before = [jnp.where(here, left[c] + tilt * start[c], before[c]) for c in range(2)]
            after = [jnp.where(here, beyond[c], after[c]) for c in range(2)]
            beyond = start

        def emit(shell, carry):
            beta, gamma = beta_ref[shell, :, cut[block]], gamma_ref[shell, :, cut[block]]
            for half in range(2):
                out_ref[shell, :, half, cut[block]] = (
                    alpha_ref[shell, half * ord_dev : (half + 1) * ord_dev, cut[block]]
                    + beta * before[half]
                    + gamma * after[half]
                )
            return carry

        lax.fori_loop(0, shells, emit, 0, unroll=2)

    for chunk in range(chunks):
        for hop in range(1, parts):
            lat_copy(chunk, hop, me).wait_send()
            back_copy(chunk, hop, me).wait_send()
    for hop in range(1, rings):
        edge_copy(hop, ring).wait_send()


def on_device(scalar_field, radial_flow, legendre, diffusivity):
    shells, ord_dev, _, degrees = scalar_field.shape
    lats = legendre.shape[2]
    parts, rings = lax.axis_size("mode"), lax.axis_size("radial")
    orders = ord_dev * parts
    modes = 2 * ord_dev
    mine = shells // parts
    synth, analysis, scale = longitude_tables(orders)
    width = 256 if lats % 256 == 0 else lats
    chunks = lats // width
    lanes, blocks = width // 128, degrees // 128
    bf16, f32 = jnp.bfloat16, jnp.float32
    vmem = pl.BlockSpec(memory_space=pltpu.VMEM)
    dma = pltpu.SemaphoreType.DMA
    return pl.pallas_call(
        functools.partial(whole_step, chunks, scale),
        in_specs=[
            pl.BlockSpec(memory_space=pltpu.SMEM),
            pl.BlockSpec(memory_space=pl.ANY),
            vmem, vmem, vmem, vmem,
        ],
        out_specs=vmem,
        out_shape=jax.ShapeDtypeStruct(scalar_field.shape, f32),
        scratch_shapes=[
            pltpu.VMEM((chunks, ord_dev, degrees, width), bf16),
            pltpu.VMEM((ord_dev, 4 * shells, degrees), bf16),
            pltpu.VMEM((lanes, 4 * shells * ord_dev, 128), f32),
            pltpu.VMEM((chunks, parts, 2, mine, modes, width), bf16),
            pltpu.VMEM((chunks, parts, 2, mine, modes, width), bf16),
            pltpu.VMEM((chunks, parts, mine, modes, width), bf16),
            pltpu.VMEM((chunks, parts, mine, modes, width), bf16),
            pltpu.VMEM((lanes, shells * modes, 128), f32),
            pltpu.VMEM((ord_dev, 2 * shells, degrees), f32),
            pltpu.VMEM((blocks, shells * modes, 128), f32),
            pltpu.VMEM((shells, modes, degrees), f32),
            pltpu.VMEM((shells, ord_dev, degrees), f32),
            pltpu.VMEM((shells, ord_dev, degrees), f32),
            pltpu.VMEM((8, ord_dev, degrees), f32),
            pltpu.VMEM((rings, 8, ord_dev, degrees), f32),
            dma((chunks,)),
            dma((chunks, parts - 1)),
            dma((chunks, parts - 1)),
            dma((chunks, parts - 1)),
            dma((chunks, parts - 1)),
            dma((rings - 1,)),
            dma((rings - 1,)),
        ],
        compiler_params=params(collective_id=0, has_side_effects=True),
        name="whole_step",
    )(diffusivity, legendre, scalar_field, radial_flow, synth, analysis)


def solution(mesh):
    return jax.shard_map(
        on_device,
        mesh=mesh,
        in_specs=(
            P("radial", "mode", None, None),
            P("radial", "mode", None, None),
            P("mode", None, None),
            P("radial"),
        ),
        out_specs=P("radial", "mode", None, None),
        check_vma=False,
    )
```

time: 707 us -> 141 us (0.20)
  loops' own time: 204 us -> 0 us
  local copies, waits for them, and re-layouts: 199 us -> 3.09 us
  Pallas kernels: 0 us -> 136 us
  other arithmetic: 103 us -> 0 us
  waiting for transfers between devices: 98.3 us -> 0 us
  matrix products: 50.1 us -> 0 us
  blocking collectives: 17.9 us -> 0 us
  starting transfers between devices: 14 us -> 0 us
  between operations: 13.7 us -> 0.01 us
    another operation x5 -> x0, loops' own time: 204 us -> none  [the longest x1 102 us: on_device(): lax.scan(sweep, (ratio_start, value_start), (diffusivity, right_side, glo...]
    pallas_call x0 -> x1, Pallas kernels: none -> 136 us  [on_device(): pl.pallas_call(functools.partial(whole_step, chunks, scale), in_specs=[pl...]
    dynamic_slice x224 -> x0, local copies, waits for them, and re-layouts: 79.9 us -> none  [on_device(): lax.scan(compose, identity, (diffusivity, right_side, global_shells))]
    dynamic_update_slice x128 -> x0, other arithmetic: 70.4 us -> none  [on_device(): lax.scan(sweep, (ratio_start, value_start), (diffusivity, right_side, glo...]
    all_to_all x3 -> x0, waiting for transfers between devices: 65.7 us -> none  [the longest x1 47.4 us: on_device(): lax.all_to_all(modes_grid, 'mode', split_axis=1, concat_axis=3, tiled=True)]
    all_to_all x6 -> x0, local copies, waits for them, and re-layouts: 53.6 us -> none  [the longest x2 24.3 us: on_device(): lax.all_to_all(flow_lat, 'mode', split_axis=3, concat_axis=1, tiled=True)]
    dot_general x5 -> x0, matrix products: 50.1 us -> none  [the longest x1 17.3 us: on_device(): jnp.einsum('rtp,mcp->rmct', product, analysis_table, preferred_element_ty...]
    all_gather x1 -> x0, waiting for transfers between devices: 32.5 us -> none  [prefix_2(): pieces = jax.tree.map(lambda part: lax.all_gather(part, axis), value)]
  transfers between devices with their start and end apart: 4 -> 0, of which waited for: 4 -> 0; matrix products, arithmetic and copies ran while one was open for 8% -> 0% of each run, Pallas kernels for 0% -> 0%
where the time goes in v2:
time: 141 us; the launch traced here: 140 us
  Pallas kernels  136 us (96%)
  local copies, waits for them, and re-layouts  3.09 us (2%)
    pallas_call x1, Pallas kernels, on_device(): pl.pallas_call(functools.partial(whole_step, chunks, scale), in_specs=[pl...  136 us
    unnamed x1, local copies, waits for them, and re-layouts  3.09 us

profile of v2, /device:TPU:1, one launch (start us, length us, event | category | flops | bytes accessed | tf_op | source)
XLA Modules:
  0.0 139.5 jit_solution(12349208029058341742)
XLA Ops:
  0.0 136.4 %whole_step.1 = f32[32,16,2,384]{3,2,1,0:T(2,128)} custom-call(f32[32]{0:T(128)} %kappa_ref.1, bf16[16,384,768]{2,1,0:T(8,128)(2,1)} %table_hbm.1, f32[32,16,2,384]{3,2,1,0:T(2,128)} %field_ref.1, f32[32,16,2,384]{3,2,1,0:T(2,128)} %flow_ref.1, bf16[256,128]{1,0:T(8,128)(2,1)} %constant.4.clone.synth_ref, bf16[128,256]{1,0:T(8,128)(2,1)} %constant.5.clone.analysis_ref), custom_call_target="tpu_custom_call" | custom-call | tf_op jit(solution)/shard_map/whole_step/pallas_call | solution.py:344
  136.4 3.1 %copy.8 = f32[32,16,2,384]{3,2,1,0:T(2,128)} copy(f32[32,16,2,384]{3,2,1,0:T(2,128)} %whole_step.1) | data formatting | bytes 3145728

commit v3 on v2

--- a/solution.py
+++ b/solution.py
@@ -36,8 +36,10 @@
 def whole_step(
     chunks, scale, kappa_ref, table_hbm, field_ref, flow_ref, synth_ref, analysis_ref, out_ref,
     table_ref, spectral_ref, rows_ref, send_ref, recv_ref, back_send_ref, back_recv_ref,
-    wide_ref, sum_ref, right_ref, alpha_ref, beta_ref, gamma_ref, edge_ref, edges_ref,
-    table_sem, send_sem, recv_sem, back_send_sem, back_recv_sem, edge_send_sem, edge_recv_sem,
+    wide_ref, sum_ref, right_ref, alpha_ref, beta_ref, gamma_ref,
+    ratio_ref, inverse_ref, slope_ref, slopes_ref, edge_ref, edges_ref,
+    table_sem, send_sem, recv_sem, back_send_sem, back_recv_sem, slope_send_sem, slope_recv_sem,
+    edge_send_sem, edge_recv_sem,
 ):
     shells, ord_dev, _, degrees = field_ref.shape
     modes = 2 * ord_dev
@@ -48,6 +50,7 @@
     width = table_ref.shape[3]
     lanes, blocks = width // 128, degrees // 128
     nr_total = shells * rings
+    group = 2 if width < 256 and mine % 2 == 0 else 1
 
     def table_copy(chunk):
         return pltpu.make_async_copy(
@@ -94,6 +97,12 @@
         return exchange(
             "radial", hop, edge_ref, edges_ref.at[slot],
             edge_send_sem.at[hop - 1], edge_recv_sem.at[hop - 1],
+        )
+
+    def slope_copy(hop, slot):
+        return exchange(
+            "radial", hop, slope_ref, slopes_ref.at[slot],
+            slope_send_sem.at[hop - 1], slope_recv_sem.at[hop - 1],
         )
 
     def stack(order, carry):
@@ -135,26 +144,93 @@
         for hop in range(1, parts):
             lat_copy(chunk, hop, me).start()
 
+    offset = nr_total * 7 // 13
+    cut = [slice(block * 128, (block + 1) * 128) for block in range(blocks)]
+    tile = (ord_dev, 128)
+    blank = jnp.zeros(tile, jnp.float32)
+    unity = jnp.ones(tile, jnp.float32)
+    angulars = []
+    for block in range(blocks):
+        degree = (
+            me * ord_dev
+            + block * 128
+            + lax.broadcasted_iota(jnp.int32, tile, 0)
+            + lax.broadcasted_iota(jnp.int32, tile, 1)
+        ).astype(jnp.float32)
+        angulars.append(degree * (degree + 1.0))
+
+    def factor(shell, carry):
+        kappa = jnp.full(tile, kappa_ref[shell], jnp.float32)
+        spot = jnp.full(tile, ring * shells + shell, jnp.int32)
+        lower = jnp.where(spot > 0, -kappa, 0.0)
+        upper = jnp.where(spot < nr_total - 1, -kappa, 0.0)
+        radius = (offset + spot).astype(jnp.float32)
+        weight = kappa / (radius * radius)
+        new = []
+        for block in range(blocks):
+            ratio, pull = carry[block]
+            diagonal = 1.0 + 2.0 * kappa + weight * angulars[block]
+            inverse = 1.0 / (diagonal - lower * ratio)
+            ratio = upper * inverse
+            pull = -lower * pull * inverse
+            inverse_ref[shell, :, cut[block]] = inverse
+            ratio_ref[shell, :, cut[block]] = ratio
+            beta_ref[shell, :, cut[block]] = pull
+            new.append((ratio, pull))
+        return tuple(new)
+
+    outset = tuple((blank, unity) for _ in range(blocks))
+    lax.fori_loop(0, shells, factor, outset)
+
+    def unfactor(step, carry):
+        shell = shells - 1 - step
+        new = []
+        for block in range(blocks):
+            beta, gamma = carry[block]
+            ratio = ratio_ref[shell, :, cut[block]]
+            beta = beta_ref[shell, :, cut[block]] - ratio * beta
+            gamma = -ratio * gamma
+            beta_ref[shell, :, cut[block]] = beta
+            gamma_ref[shell, :, cut[block]] = gamma
+            new.append((beta, gamma))
+        return tuple(new)
+
+    lax.fori_loop(0, shells, unfactor, outset)
+    for side, shell in enumerate((0, shells - 1)):
+        slope_ref[2 * side] = beta_ref[shell]
+        slope_ref[2 * side + 1] = gamma_ref[shell]
+    slopes_ref[ring] = slope_ref[...]
+    for hop in range(1, rings):
+        slope_copy(hop, ring).start()
+
     for chunk in range(chunks):
         for hop in range(1, parts):
             lat_copy(chunk, hop, lax.rem(me + parts - hop, parts)).wait_recv()
 
-        def multiply(local, carry):
+        def multiply(step, carry):
+            locals_ = [step * group + k for k in range(group)]
             grids = []
             for which in range(2):
                 lat = jnp.concatenate(
-                    [recv_ref[chunk, part, which, local] for part in range(parts)], axis=0
+                    [
+                        jnp.concatenate(
+                            [recv_ref[chunk, part, which, local] for part in range(parts)], axis=0
+                        )
+                        for local in locals_
+                    ],
+                    axis=1,
                 )
                 grids.append(jnp.dot(synth_ref[...], lat, preferred_element_type=jnp.float32))
             product = (grids[0] * grids[1]).astype(jnp.bfloat16)
             back = jnp.dot(analysis_ref[...], product, preferred_element_type=jnp.float32) * scale
-            for part in range(parts):
-                back_send_ref[chunk, part, local] = back[part * modes : (part + 1) * modes].astype(
-                    jnp.bfloat16
-                )
-            return carry
-
-        lax.fori_loop(0, mine, multiply, 0)
+            for k, local in enumerate(locals_):
+                for part in range(parts):
+                    back_send_ref[chunk, part, local] = back[
+                        part * modes : (part + 1) * modes, k * width : (k + 1) * width
+                    ].astype(jnp.bfloat16)
+            return carry
+
+        lax.fori_loop(0, mine // group, multiply, 0)
         back_recv_ref[chunk, me] = back_send_ref[chunk, me]
         for hop in range(1, parts):
             back_copy(chunk, hop, me).start()
@@ -208,78 +284,49 @@
 
         lax.fori_loop(0, ord_dev, untransform, 0, unroll=2)
 
-    offset = nr_total * 7 // 13
-    cut = [slice(block * 128, (block + 1) * 128) for block in range(blocks)]
-    tile = (ord_dev, 128)
-    angulars = []
-    for block in range(blocks):
-        degree = (
-            me * ord_dev
-            + block * 128
-            + lax.broadcasted_iota(jnp.int32, tile, 0)
-            + lax.broadcasted_iota(jnp.int32, tile, 1)
-        ).astype(jnp.float32)
-        angulars.append(degree * (degree + 1.0))
-
     def forward(shell, carry):
         index = ring * shells + shell
-        kappa = jnp.full(tile, kappa_ref[shell], jnp.float32)
-        spot = jnp.full(tile, index, jnp.int32)
-        lower = jnp.where(spot > 0, -kappa, 0.0)
-        upper = jnp.where(spot < nr_total - 1, -kappa, 0.0)
-        radius = (offset + spot).astype(jnp.float32)
-        weight = kappa / (radius * radius)
+        lower = jnp.where(jnp.full(tile, index, jnp.int32) > 0, -kappa_ref[shell], 0.0)
         start = pl.multiple_of(shell * modes, modes)
         new = []
         for block in range(blocks):
-            ratio, value0, value1, pull = carry[block]
-            diagonal = 1.0 + 2.0 * kappa + weight * angulars[block]
-            inverse = 1.0 / (diagonal - lower * ratio)
-            ratio = upper * inverse
-            value0 = (right_ref[block, pl.ds(start, ord_dev), :] - lower * value0) * inverse
+            inverse = inverse_ref[shell, :, cut[block]]
+            value0 = (
+                right_ref[block, pl.ds(start, ord_dev), :] - lower * carry[block][0]
+            ) * inverse
             value1 = (
-                right_ref[block, pl.ds(start + ord_dev, ord_dev), :] - lower * value1
+                right_ref[block, pl.ds(start + ord_dev, ord_dev), :] - lower * carry[block][1]
             ) * inverse
-            pull = -lower * pull * inverse
             alpha_ref[shell, :ord_dev, cut[block]] = value0
             alpha_ref[shell, ord_dev:, cut[block]] = value1
-            beta_ref[shell, :, cut[block]] = pull
-            gamma_ref[shell, :, cut[block]] = ratio
-            new.append((ratio, value0, value1, pull))
+            new.append((value0, value1))
         return tuple(new)
 
-    blank = jnp.zeros(tile, jnp.float32)
-    unity = jnp.ones(tile, jnp.float32)
-    outset = tuple((blank, blank, blank, unity) for _ in range(blocks))
-    lax.fori_loop(0, shells, forward, outset)
+    empty = tuple((blank, blank) for _ in range(blocks))
+    lax.fori_loop(0, shells, forward, empty, unroll=4)
 
     def backward(step, carry):
         shell = shells - 1 - step
         new = []
         for block in range(blocks):
-            alpha0, alpha1, beta, gamma = carry[block]
-            ratio = gamma_ref[shell, :, cut[block]]
-            alpha0 = alpha_ref[shell, :ord_dev, cut[block]] - ratio * alpha0
-            alpha1 = alpha_ref[shell, ord_dev:, cut[block]] - ratio * alpha1
-            beta = beta_ref[shell, :, cut[block]] - ratio * beta
-            gamma = -ratio * gamma
+            ratio = ratio_ref[shell, :, cut[block]]
+            alpha0 = alpha_ref[shell, :ord_dev, cut[block]] - ratio * carry[block][0]
+            alpha1 = alpha_ref[shell, ord_dev:, cut[block]] - ratio * carry[block][1]
             alpha_ref[shell, :ord_dev, cut[block]] = alpha0
             alpha_ref[shell, ord_dev:, cut[block]] = alpha1
-            beta_ref[shell, :, cut[block]] = beta
-            gamma_ref[shell, :, cut[block]] = gamma
-            new.append((alpha0, alpha1, beta, gamma))
+            new.append((alpha0, alpha1))
         return tuple(new)
 
-    lax.fori_loop(0, shells, backward, outset)
+    lax.fori_loop(0, shells, backward, empty, unroll=4)
 
     for side, shell in enumerate((0, shells - 1)):
-        edge_ref[4 * side] = alpha_ref[shell, :ord_dev]
-        edge_ref[4 * side + 1] = alpha_ref[shell, ord_dev:]
-        edge_ref[4 * side + 2] = beta_ref[shell]
-        edge_ref[4 * side + 3] = gamma_ref[shell]
+        edge_ref[2 * side] = alpha_ref[shell, :ord_dev]
+        edge_ref[2 * side + 1] = alpha_ref[shell, ord_dev:]
     edges_ref[ring] = edge_ref[...]
     for hop in range(1, rings):
         edge_copy(hop, ring).start()
+    for hop in range(1, rings):
+        slope_copy(hop, lax.rem(ring + rings - hop, rings)).wait_recv()
     for hop in range(1, rings):
         edge_copy(hop, lax.rem(ring + rings - hop, rings)).wait_recv()
 
@@ -288,8 +335,8 @@
         known, slope = [blank, blank], blank
         lefts, firsts = [], []
         for device in range(rings):
-            head = [edges_ref[device, k, :, cut[block]] for k in range(4)]
-            tail = [edges_ref[device, 4 + k, :, cut[block]] for k in range(4)]
+            head = [ref[device, k, :, cut[block]] for ref in (edges_ref, slopes_ref) for k in (0, 1)]
+            tail = [ref[device, k, :, cut[block]] for ref in (edges_ref, slopes_ref) for k in (2, 3)]
             lefts.append((known, slope))
             inverse = 1.0 / (1.0 - head[2] * slope)
             const = [(head[c] + head[2] * known[c]) * inverse for c in range(2)]
@@ -324,6 +371,7 @@
             lat_copy(chunk, hop, me).wait_send()
             back_copy(chunk, hop, me).wait_send()
     for hop in range(1, rings):
+        slope_copy(hop, ring).wait_send()
         edge_copy(hop, ring).wait_send()
 
 
@@ -335,7 +383,7 @@
     modes = 2 * ord_dev
     mine = shells // parts
     synth, analysis, scale = longitude_tables(orders)
-    width = 256 if lats % 256 == 0 else lats
+    width = 128 if lats % 128 == 0 else lats
     chunks = lats // width
     lanes, blocks = width // 128, degrees // 128
     bf16, f32 = jnp.bfloat16, jnp.float32
@@ -364,13 +412,19 @@
             pltpu.VMEM((shells, modes, degrees), f32),
             pltpu.VMEM((shells, ord_dev, degrees), f32),
             pltpu.VMEM((shells, ord_dev, degrees), f32),
-            pltpu.VMEM((8, ord_dev, degrees), f32),
-            pltpu.VMEM((rings, 8, ord_dev, degrees), f32),
+            pltpu.VMEM((shells, ord_dev, degrees), f32),
+            pltpu.VMEM((shells, ord_dev, degrees), f32),
+            pltpu.VMEM((4, ord_dev, degrees), f32),
+            pltpu.VMEM((rings, 4, ord_dev, degrees), f32),
+            pltpu.VMEM((4, ord_dev, degrees), f32),
+            pltpu.VMEM((rings, 4, ord_dev, degrees), f32),
             dma((chunks,)),
             dma((chunks, parts - 1)),
             dma((chunks, parts - 1)),
             dma((chunks, parts - 1)),
             dma((chunks, parts - 1)),
+            dma((rings - 1,)),
+            dma((rings - 1,)),
             dma((rings - 1,)),
             dma((rings - 1,)),
         ],

time: 141 us -> 130 us (0.922); the launches traced: 140 us -> 130 us
  Pallas kernels: 136 us -> 127 us
    pallas_call x1, Pallas kernels: 136 us -> 127 us  [on_device(): pl.pallas_call(functools.partial(whole_step, chunks, scale), in_specs=[pl...]
where the time goes in v3:
time: 130 us
  Pallas kernels  127 us (98%)
  local copies, waits for them, and re-layouts  3.09 us (2%)
    pallas_call x1, Pallas kernels, on_device(): pl.pallas_call(functools.partial(whole_step, chunks, scale), in_specs=[pl...  127 us
    unnamed x1, local copies, waits for them, and re-layouts  3.09 us

profile of v3, /device:TPU:1, one launch (start us, length us, event | category | flops | bytes accessed | tf_op | source)
XLA Modules:
  0.0 130.1 jit_solution(16880663881086530196)
XLA Ops:
  0.0 127.0 %whole_step.1 = f32[32,16,2,384]{3,2,1,0:T(2,128)} custom-call(f32[32]{0:T(128)} %kappa_ref.1, bf16[16,384,768]{2,1,0:T(8,128)(2,1)} %table_hbm.1, f32[32,16,2,384]{3,2,1,0:T(2,128)} %field_ref.1, f32[32,16,2,384]{3,2,1,0:T(2,128)} %flow_ref.1, bf16[256,128]{1,0:T(8,128)(2,1)} %constant.4.clone.synth_ref, bf16[128,256]{1,0:T(8,128)(2,1)} %constant.5.clone.analysis_ref), custom_call_target="tpu_custom_call" | custom-call | tf_op jit(solution)/shard_map/whole_step/pallas_call | solution.py:392
  127.0 3.1 %copy.8 = f32[32,16,2,384]{3,2,1,0:T(2,128)} copy(f32[32,16,2,384]{3,2,1,0:T(2,128)} %whole_step.1) | data formatting | bytes 3145728

commit v4 on v3

--- a/solution.py
+++ b/solution.py
@@ -31,6 +31,14 @@
     synth = (paired / np.float32(math.sqrt(orders))).astype(jnp.bfloat16)
     analysis = (paired * np.float32(math.sqrt(2.0 / NLON))).astype(jnp.bfloat16)
     return jnp.asarray(synth.T), jnp.asarray(analysis), float(stride)
+
+
+def partner(here, hop, size):
+    place, bit = 0, 1
+    while bit < size:
+        place = place + (here // bit + hop // bit) % 2 * bit
+        bit *= 2
+    return place
 
 
 def whole_step(
@@ -63,45 +71,44 @@
     barrier = pltpu.get_barrier_semaphore()
     for hop in range(1, parts):
         pl.semaphore_signal(
-            barrier, inc=1, device_id={"mode": lax.rem(me + hop, parts)},
+            barrier, inc=1, device_id={"mode": partner(me, hop, parts)},
             device_id_type=pl.DeviceIdType.MESH,
         )
     for hop in range(1, rings):
         pl.semaphore_signal(
-            barrier, inc=1, device_id={"radial": lax.rem(ring + hop, rings)},
+            barrier, inc=1, device_id={"radial": partner(ring, hop, rings)},
             device_id_type=pl.DeviceIdType.MESH,
         )
 
-    def exchange(axis, hop, source, target, send, receive):
-        here, size = (me, parts) if axis == "mode" else (ring, rings)
+    def exchange(axis, to, source, target, send, receive):
         return pltpu.make_async_remote_copy(
             src_ref=source, dst_ref=target, send_sem=send, recv_sem=receive,
-            device_id={axis: lax.rem(here + hop, size)}, device_id_type=pl.DeviceIdType.MESH,
+            device_id={axis: to}, device_id_type=pl.DeviceIdType.MESH,
         )
 
     def lat_copy(chunk, hop, slot):
-        to = lax.rem(me + hop, parts)
+        to = partner(me, hop, parts)
         return exchange(
-            "mode", hop, send_ref.at[chunk, to], recv_ref.at[chunk, slot],
+            "mode", to, send_ref.at[chunk, to], recv_ref.at[chunk, slot],
             send_sem.at[chunk, hop - 1], recv_sem.at[chunk, hop - 1],
         )
 
     def back_copy(chunk, hop, slot):
-        to = lax.rem(me + hop, parts)
+        to = partner(me, hop, parts)
         return exchange(
-            "mode", hop, back_send_ref.at[chunk, to], back_recv_ref.at[chunk, slot],
+            "mode", to, back_send_ref.at[chunk, to], back_recv_ref.at[chunk, slot],
             back_send_sem.at[chunk, hop - 1], back_recv_sem.at[chunk, hop - 1],
         )
 
     def edge_copy(hop, slot):
         return exchange(
-            "radial", hop, edge_ref, edges_ref.at[slot],
+            "radial", partner(ring, hop, rings), edge_ref, edges_ref.at[slot],
             edge_send_sem.at[hop - 1], edge_recv_sem.at[hop - 1],
         )
 
     def slope_copy(hop, slot):
         return exchange(
-            "radial", hop, slope_ref, slopes_ref.at[slot],
+            "radial", partner(ring, hop, rings), slope_ref, slopes_ref.at[slot],
             slope_send_sem.at[hop - 1], slope_recv_sem.at[hop - 1],
         )
 
@@ -141,7 +148,12 @@
         recv_ref[chunk, me] = send_ref[chunk, me]
         if chunk == 0:
             pl.semaphore_wait(barrier, parts + rings - 2)
-        for hop in range(1, parts):
+        near = parts if chunk < 2 else parts // 2
+        for hop in range(1, near):
+            lat_copy(chunk, hop, me).start()
+
+    for chunk in range(2, chunks):
+        for hop in range(parts // 2, parts):
             lat_copy(chunk, hop, me).start()
 
     offset = nr_total * 7 // 13
@@ -205,7 +217,7 @@
 
     for chunk in range(chunks):
         for hop in range(1, parts):
-            lat_copy(chunk, hop, lax.rem(me + parts - hop, parts)).wait_recv()
+            lat_copy(chunk, hop, partner(me, hop, parts)).wait_recv()
 
         def multiply(step, carry):
             locals_ = [step * group + k for k in range(group)]
@@ -237,7 +249,7 @@
 
     for chunk in range(chunks):
         for hop in range(1, parts):
-            back_copy(chunk, hop, lax.rem(me + parts - hop, parts)).wait_recv()
+            back_copy(chunk, hop, partner(me, hop, parts)).wait_recv()
 
         def widen(shell, carry):
             base = pl.multiple_of(shell * modes, modes)
@@ -326,9 +338,9 @@
     for hop in range(1, rings):
         edge_copy(hop, ring).start()
     for hop in range(1, rings):
-        slope_copy(hop, lax.rem(ring + rings - hop, rings)).wait_recv()
-    for hop in range(1, rings):
-        edge_copy(hop, lax.rem(ring + rings - hop, rings)).wait_recv()
+        slope_copy(hop, partner(ring, hop, rings)).wait_recv()
+    for hop in range(1, rings):
+        edge_copy(hop, partner(ring, hop, rings)).wait_recv()
 
     spot = jnp.full(tile, ring, jnp.int32)
     for block in range(blocks):
@@ -382,6 +394,7 @@
     orders = ord_dev * parts
     modes = 2 * ord_dev
     mine = shells // parts
+    assert parts & (parts - 1) == 0 and rings & (rings - 1) == 0
     synth, analysis, scale = longitude_tables(orders)
     width = 128 if lats % 128 == 0 else lats
     chunks = lats // width

time: 130 us -> 131 us (level)
  no operation moved by 1% of the time
where the time goes in v4:
time: 131 us
  Pallas kernels  128 us (98%)
  local copies, waits for them, and re-layouts  3.09 us (2%)
    pallas_call x1, Pallas kernels, on_device(): pl.pallas_call(functools.partial(whole_step, chunks, scale), in_specs=[pl...  128 us
    unnamed x1, local copies, waits for them, and re-layouts  3.09 us

profile of v4, /device:TPU:1, one launch (start us, length us, event | category | flops | bytes accessed | tf_op | source)
XLA Modules:
  0.0 131.2 jit_solution(8182413422916361515)
XLA Ops:
  0.0 128.1 %whole_step.1 = f32[32,16,2,384]{3,2,1,0:T(2,128)} custom-call(f32[32]{0:T(128)} %kappa_ref.1, bf16[16,384,768]{2,1,0:T(8,128)(2,1)} %table_hbm.1, f32[32,16,2,384]{3,2,1,0:T(2,128)} %field_ref.1, f32[32,16,2,384]{3,2,1,0:T(2,128)} %flow_ref.1, bf16[256,128]{1,0:T(8,128)(2,1)} %constant.4.clone.synth_ref, bf16[128,256]{1,0:T(8,128)(2,1)} %constant.5.clone.analysis_ref), custom_call_target="tpu_custom_call" | custom-call | tf_op jit(solution)/shard_map/whole_step/pallas_call | solution.py:405
  128.1 3.1 %copy.8 = f32[32,16,2,384]{3,2,1,0:T(2,128)} copy(f32[32,16,2,384]{3,2,1,0:T(2,128)} %whole_step.1) | data formatting | bytes 3145728

commit v5 on v3

--- a/solution.py
+++ b/solution.py
@@ -31,6 +31,14 @@
     synth = (paired / np.float32(math.sqrt(orders))).astype(jnp.bfloat16)
     analysis = (paired * np.float32(math.sqrt(2.0 / NLON))).astype(jnp.bfloat16)
     return jnp.asarray(synth.T), jnp.asarray(analysis), float(stride)
+
+
+def partner(here, hop, size):
+    place, bit = 0, 1
+    while bit < size:
+        place = place + (here // bit + hop // bit) % 2 * bit
+        bit *= 2
+    return place
 
 
 def whole_step(
@@ -94,9 +102,13 @@
         )
 
     def edge_copy(hop, slot):
-        return exchange(
-            "radial", hop, edge_ref, edges_ref.at[slot],
-            edge_send_sem.at[hop - 1], edge_recv_sem.at[hop - 1],
+        relayed = hop > 1 and hop % 2 == 1
+        source = edges_ref.at[partner(ring, hop - 1, rings)] if relayed else edge_ref
+        return pltpu.make_async_remote_copy(
+            src_ref=source, dst_ref=edges_ref.at[slot],
+            send_sem=edge_send_sem.at[hop - 1], recv_sem=edge_recv_sem.at[hop - 1],
+            device_id={"radial": partner(ring, 1 if relayed else hop, rings)},
+            device_id_type=pl.DeviceIdType.MESH,
         )
 
     def slope_copy(hop, slot):
@@ -323,27 +335,47 @@
         edge_ref[2 * side] = alpha_ref[shell, :ord_dev]
         edge_ref[2 * side + 1] = alpha_ref[shell, ord_dev:]
     edges_ref[ring] = edge_ref[...]
-    for hop in range(1, rings):
+    direct = [hop for hop in range(1, rings) if hop == 1 or hop % 2 == 0]
+    for hop in reversed(direct):
         edge_copy(hop, ring).start()
     for hop in range(1, rings):
         slope_copy(hop, lax.rem(ring + rings - hop, rings)).wait_recv()
-    for hop in range(1, rings):
-        edge_copy(hop, lax.rem(ring + rings - hop, rings)).wait_recv()
+
+    factors = []
+    for block in range(blocks):
+        slope, steps = blank, []
+        for device in range(rings):
+            head0, head1, tail0, tail1 = [slopes_ref[device, k, :, cut[block]] for k in range(4)]
+            inverse = 1.0 / (1.0 - head0 * slope)
+            gain = head1 * inverse
+            steps.append((inverse, gain, slope))
+            slope = tail1 + tail0 * slope * gain
+        factors.append(steps)
+
+    for hop in direct:
+        edge_copy(hop, partner(ring, hop, rings)).wait_recv()
+        if hop % 2 == 0:
+            edge_copy(hop + 1, partner(ring, hop, rings)).start()
+    for hop in range(3, rings, 2):
+        edge_copy(hop, partner(ring, hop, rings)).wait_recv()
 
     spot = jnp.full(tile, ring, jnp.int32)
     for block in range(blocks):
-        known, slope = [blank, blank], blank
+        known = [blank, blank]
         lefts, firsts = [], []
         for device in range(rings):
-            head = [ref[device, k, :, cut[block]] for ref in (edges_ref, slopes_ref) for k in (0, 1)]
-            tail = [ref[device, k, :, cut[block]] for ref in (edges_ref, slopes_ref) for k in (2, 3)]
+            inverse, gain, slope = factors[block][device]
+            head = slopes_ref[device, 0, :, cut[block]]
+            tail = slopes_ref[device, 2, :, cut[block]]
             lefts.append((known, slope))
-            inverse = 1.0 / (1.0 - head[2] * slope)
-            const = [(head[c] + head[2] * known[c]) * inverse for c in range(2)]
-            gain = head[3] * inverse
+            const = [
+                (edges_ref[device, c, :, cut[block]] + head * known[c]) * inverse for c in range(2)
+            ]
             firsts.append((const, gain))
-            known = [tail[c] + tail[2] * (known[c] + slope * const[c]) for c in range(2)]
-            slope = tail[3] + tail[2] * slope * gain
+            known = [
+                edges_ref[device, 2 + c, :, cut[block]] + tail * (known[c] + slope * const[c])
+                for c in range(2)
+            ]
         beyond, before, after = [blank, blank], [blank, blank], [blank, blank]
         for device in reversed(range(rings)):
             const, gain = firsts[device]
@@ -382,6 +414,7 @@
     orders = ord_dev * parts
     modes = 2 * ord_dev
     mine = shells // parts
+    assert rings & (rings - 1) == 0
     synth, analysis, scale = longitude_tables(orders)
     width = 128 if lats % 128 == 0 else lats
     chunks = lats // width

time: 130 us -> 128 us (0.985)
  Pallas kernels: 127 us -> 125 us
    pallas_call x1, Pallas kernels: 127 us -> 125 us  [on_device(): pl.pallas_call(functools.partial(whole_step, chunks, scale), in_specs=[pl...]
where the time goes in v5:
time: 128 us
  Pallas kernels  125 us (98%)
  local copies, waits for them, and re-layouts  3.09 us (2%)
    pallas_call x1, Pallas kernels, on_device(): pl.pallas_call(functools.partial(whole_step, chunks, scale), in_specs=[pl...  125 us
    unnamed x1, local copies, waits for them, and re-layouts  3.09 us

profile of v5, /device:TPU:1, one launch (start us, length us, event | category | flops | bytes accessed | tf_op | source)
XLA Modules:
  0.0 127.8 jit_solution(7271373857334394641)
XLA Ops:
  0.0 124.7 %whole_step.1 = f32[32,16,2,384]{3,2,1,0:T(2,128)} custom-call(f32[32]{0:T(128)} %kappa_ref.1, bf16[16,384,768]{2,1,0:T(8,128)(2,1)} %table_hbm.1, f32[32,16,2,384]{3,2,1,0:T(2,128)} %field_ref.1, f32[32,16,2,384]{3,2,1,0:T(2,128)} %flow_ref.1, bf16[256,128]{1,0:T(8,128)(2,1)} %constant.4.clone.synth_ref, bf16[128,256]{1,0:T(8,128)(2,1)} %constant.5.clone.analysis_ref), custom_call_target="tpu_custom_call" | custom-call | tf_op jit(solution)/shard_map/whole_step/pallas_call | solution.py:425
  124.8 3.1 %copy.8 = f32[32,16,2,384]{3,2,1,0:T(2,128)} copy(f32[32,16,2,384]{3,2,1,0:T(2,128)} %whole_step.1) | data formatting | bytes 3145728

commit v6 on v5

--- a/solution.py
+++ b/solution.py
@@ -123,7 +123,7 @@
         ).astype(jnp.bfloat16)
         return carry
 
-    lax.fori_loop(0, ord_dev, stack, 0, unroll=2)
+    lax.fori_loop(0, ord_dev, stack, 0, unroll=4)
 
     for chunk in range(chunks):
         table_copy(chunk).wait()
@@ -137,7 +137,7 @@
                 rows_ref[lane, pl.ds(base, count), :] = lat[:, lane * 128 : (lane + 1) * 128]
             return carry
 
-        lax.fori_loop(0, ord_dev, transform, 0, unroll=2)
+        lax.fori_loop(0, ord_dev, transform, 0, unroll=4)
 
         def pack(row, carry):
             which, shell = row // shells, row % shells
@@ -149,7 +149,7 @@
                 )
             return carry
 
-        lax.fori_loop(0, 2 * shells, pack, 0, unroll=4)
+        lax.fori_loop(0, 2 * shells, pack, 0, unroll=8)
         recv_ref[chunk, me] = send_ref[chunk, me]
         if chunk == 0:
             pl.semaphore_wait(barrier, parts + rings - 2)
@@ -242,7 +242,7 @@
                     ].astype(jnp.bfloat16)
             return carry
 
-        lax.fori_loop(0, mine // group, multiply, 0)
+        lax.fori_loop(0, mine // group, multiply, 0, unroll=2)
         back_recv_ref[chunk, me] = back_send_ref[chunk, me]
         for hop in range(1, parts):
             back_copy(chunk, hop, me).start()
@@ -294,7 +294,7 @@
                     ]
             return carry
 
-        lax.fori_loop(0, ord_dev, untransform, 0, unroll=2)
+        lax.fori_loop(0, ord_dev, untransform, 0, unroll=4)
 
     def forward(shell, carry):
         index = ring * shells + shell
@@ -396,7 +396,7 @@
                 )
             return carry
 
-        lax.fori_loop(0, shells, emit, 0, unroll=2)
+        lax.fori_loop(0, shells, emit, 0, unroll=4)
 
     for chunk in range(chunks):
         for hop in range(1, parts):

time: 128 us -> 127 us (level)
  no operation moved by 1% of the time
where the time goes in v6:
time: 127 us
  Pallas kernels  124 us (98%)
  local copies, waits for them, and re-layouts  3.09 us (2%)
    pallas_call x1, Pallas kernels, on_device(): pl.pallas_call(functools.partial(whole_step, chunks, scale), in_specs=[pl...  124 us
    unnamed x1, local copies, waits for them, and re-layouts  3.09 us

profile of v6, /device:TPU:1, one launch (start us, length us, event | category | flops | bytes accessed | tf_op | source)
XLA Modules:
  0.0 126.8 jit_solution(10498689993048730129)
XLA Ops:
  0.0 123.7 %whole_step.1 = f32[32,16,2,384]{3,2,1,0:T(2,128)} custom-call(f32[32]{0:T(128)} %kappa_ref.1, bf16[16,384,768]{2,1,0:T(8,128)(2,1)} %table_hbm.1, f32[32,16,2,384]{3,2,1,0:T(2,128)} %field_ref.1, f32[32,16,2,384]{3,2,1,0:T(2,128)} %flow_ref.1, bf16[256,128]{1,0:T(8,128)(2,1)} %constant.4.clone.synth_ref, bf16[128,256]{1,0:T(8,128)(2,1)} %constant.5.clone.analysis_ref), custom_call_target="tpu_custom_call" | custom-call | tf_op jit(solution)/shard_map/whole_step/pallas_call | solution.py:425
  123.7 3.1 %copy.8 = f32[32,16,2,384]{3,2,1,0:T(2,128)} copy(f32[32,16,2,384]{3,2,1,0:T(2,128)} %whole_step.1) | data formatting | bytes 3145728
